TPU v7x, 128 devices: a whole 4x4x4 slice. The times are simulated.
128 devices in a mesh: dp: 16 (over x_lo, z, core), chan: 8 (over y, x_hi).
Axes of the slice: x: 4 (x_hi: 2, x_lo: 2; x = x_hi * 2 + x_lo), y: 4, z: 4, core: 2. Of those that a mesh axis runs over, the one named last changes fastest.
Arguments:
- volume: bfloat16 [16, 512, 1024], P('dp', 'chan'), may hold values from -16 to 16
- w_first: bfloat16 [27, 512, 512], P(None, 'chan'), may hold values from -0.0546875 to 0.0546875
- gain: float32 [512], replicated, may hold values from 0.1 to 1.9
- w_second: bfloat16 [27, 512, 512], P(None, None, 'chan'), may hold values from -0.0546875 to 0.0546875
- cotangent: bfloat16 [16, 512, 1024], P('dp', 'chan'), may hold values from -8 to 8
Outputs:
- output: bfloat16 [16, 512, 1024], P('dp', 'chan')
- grad_volume: bfloat16 [16, 512, 1024], P('dp', 'chan')
- grad_w_first: float32 [27, 512, 512], P(None, 'chan')
- grad_gain: float32 [512], P('chan')
- grad_w_second: float32 [27, 512, 512], P(None, None, 'chan')
All inputs are finite; a program needn't handle non-finite values.
Results may differ from a plain program's by a relative error of at most 0.005.
Values may be sent and summed in bfloat16 or wider, within the bound.
A program may use at most 64 MiB of HBM per device.

v0:
```python
import math
import jax
import jax.numpy as jnp
from jax import lax
from jax.sharding import PartitionSpec as P

DEPTH = 4
HEIGHT = 16
WIDTH = 16
TAP_OFFSETS = [
    (plane_off, row_off, col_off)
    for plane_off in (-1, 0, 1)
    for row_off in (-1, 0, 1)
    for col_off in (-1, 0, 1)
]
NORM_EPS = 1e-05


def moved_cells(field, plane_off, row_off, col_off):
    cell_count = field.shape[1]
    plane_cells = HEIGHT * WIDTH
    offset = plane_off * plane_cells + row_off * WIDTH + col_off
    margin = plane_cells + WIDTH + 1
    padded = jnp.pad(field, ((0, 0), (margin, margin)))
    sliced = lax.slice_in_dim(padded, margin + offset, margin + offset + cell_count, axis=1)
    cells = jnp.arange(cell_count, dtype=jnp.int32)
    depth_at = cells // plane_cells + plane_off
    row_at = cells // WIDTH % HEIGHT + row_off
    col_at = cells % WIDTH + col_off
    inside = (
        (depth_at >= 0)
        & (depth_at < DEPTH)
        & (row_at >= 0)
        & (row_at < HEIGHT)
        & (col_at >= 0)
        & (col_at < WIDTH)
    )
    return jnp.where(inside[None, :], sliced, jnp.zeros_like(sliced))


def stack_taps(field, sign):
    layers = [
        moved_cells(field, sign * offsets[0], sign * offsets[1], sign * offsets[2])
        for offsets in TAP_OFFSETS
    ]
    return jnp.concatenate(layers, axis=0).reshape(27, field.shape[0], field.shape[1])


def block_rows(count):
    chosen = 1
    for trial in range(1, 65):
        if count % trial == 0:
            chosen = trial
    return chosen


def normalize(pre, gain_rows):
    center = pre - jnp.mean(pre, axis=1, keepdims=True)
    inverse = lax.rsqrt(jnp.mean(center * center, axis=1, keepdims=True) + NORM_EPS)
    normed = center * inverse
    scaled = gain_rows[:, None] * normed
    return (normed, inverse, scaled, jax.nn.silu(scaled).astype(jnp.bfloat16))


def normalize_back(dact, normed, inverse, scaled, gain_rows):
    sigma = jax.nn.sigmoid(scaled)
    dscaled = dact * sigma * (1.0 + scaled * (1.0 - sigma))
    gain_part = jnp.sum(dscaled * normed, axis=1)
    dnormed = dscaled * gain_rows[:, None]
    dpre = (
        dnormed
        - jnp.mean(dnormed, axis=1, keepdims=True)
        - normed * jnp.mean(dnormed * normed, axis=1, keepdims=True)
    ) * inverse
    return (gain_part, dpre.astype(jnp.bfloat16))


def shards(volume, w_first, gain, w_second, cotangent):
    local_rows = volume.shape[1]
    channels_all = w_first.shape[2]
    cell_count = volume.shape[2]
    source = volume[0]
    target = cotangent[0]
    chan_index = lax.axis_index("chan")
    volume_cols = stack_taps(source, 1)
    target_cols = stack_taps(target, -1)
    contract_first = (((0, 1), (0, 1)), ((), ()))
    contract_second = (((0, 2), (0, 1)), ((), ()))
    contract_cells = (((2,), (1,)), ((), ()))
    second_init = (
        jnp.zeros((local_rows, cell_count), jnp.float32),
        jnp.zeros((27, channels_all, local_rows), jnp.float32),
    )
    first_init = (
        jnp.zeros((local_rows, cell_count), jnp.float32),
        jnp.zeros((27, local_rows, channels_all), jnp.float32),
    )
    own_gain = lax.dynamic_slice_in_dim(gain, chan_index * local_rows, local_rows, 0)
    weights = w_first
    pre_own = lax.psum_scatter(
        lax.dot_general(weights, volume_cols, contract_first, preferred_element_type=jnp.float32),
        "chan",
        scatter_dimension=0,
        tiled=True,
    )
    normed, inverse, scaled, act_own = normalize(pre_own, own_gain)
    act_rows = lax.all_gather(act_own, "chan", axis=0, tiled=True)
    count = act_rows.shape[0]
    step_rows = block_rows(count)

    def second_one_block(index, inner):
        out_now, grad_now = inner
        begin = index * step_rows
        rows = lax.dynamic_slice_in_dim(act_rows, begin, step_rows, 0)
        cols = stack_taps(rows, 1)
        weights = lax.dynamic_slice_in_dim(w_second, begin, step_rows, 1)
        out_now = out_now + lax.dot_general(
            weights, cols, contract_first, preferred_element_type=jnp.float32
        )
        grad_part = lax.dot_general(
            cols, target, contract_cells, preferred_element_type=jnp.float32
        )
        grad_now = lax.dynamic_update_slice_in_dim(grad_now, grad_part, begin, 1)
        return (out_now, grad_now)

    out_sum, second_grad = lax.fori_loop(0, count // step_rows, second_one_block, second_init)
    output = out_sum.astype(jnp.bfloat16)[None]
    factor = 1.0 / math.sqrt(lax.axis_size("dp") * cell_count)
    weights = w_second
    dact_own = lax.psum_scatter(
        lax.dot_general(weights, target_cols, contract_second, preferred_element_type=jnp.float32),
        "chan",
        scatter_dimension=0,
        tiled=True,
    )
    gain_part, dpre_own = normalize_back(dact_own, normed, inverse, scaled, own_gain)
    grad_rows = lax.all_gather(dpre_own, "chan", axis=0, tiled=True)
    count = grad_rows.shape[0]
    first_step_rows = block_rows(count)

    def first_one_block(index, inner):
        back_now, grad_now = inner
        begin = index * first_step_rows
        rows = lax.dynamic_slice_in_dim(grad_rows, begin, first_step_rows, 0)
        cols = stack_taps(rows, -1)
        weights = lax.dynamic_slice_in_dim(w_first, begin, first_step_rows, 2)
        back_now = back_now + lax.dot_general(
            weights, cols, contract_second, preferred_element_type=jnp.float32
        )
        grad_part = lax.dot_general(
            volume_cols, rows, contract_cells, preferred_element_type=jnp.float32
        )
        grad_now = lax.dynamic_update_slice_in_dim(grad_now, grad_part, begin, 2)
        return (back_now, grad_now)

    back_sum, first_grad = lax.fori_loop(0, count // first_step_rows, first_one_block, first_init)
    first_total, second_total, gain_total = lax.psum((first_grad, second_grad, gain_part), "dp")
    grad_volume = back_sum.astype(jnp.bfloat16)[None]
    return (output, grad_volume, first_total * factor, gain_total * factor, second_total * factor)


def solution(mesh):
    placed = (
        P("dp", "chan", None),
        P(None, "chan", None),
        P(),
        P(None, None, "chan"),
        P("dp", "chan", None),
    )
    return jax.shard_map(
        shards,
        mesh=mesh,
        in_specs=placed,
        out_specs=(
            P("dp", "chan", None),
            P("dp", "chan", None),
            P(None, "chan", None),
            P("chan"),
            P(None, None, "chan"),
        ),
        check_vma=False,
    )
```

profile of v0, /device:TPU:0, one launch (start us, length us, event | category | flops | bytes accessed | tf_op | source)
XLA Modules:
  0.0 805.6 jit_solution(12205179865725809057)
XLA Ops:
  32.9 6.0 convolution_bitcast_fusion.3
  42.5 67.8 %reduce-scatter.7.cloned.1.call-done = f32[64,1024]{1,0:T(8,128)} async-done(((f32[512,1024]{1,0:T(8,128)}), f32[64,1024]{1,0:T(8,128)}) %reduce-scatter.7.cloned.1.call-update) | async-done | bytes 262160 | tf_op jit(solution)/shard_map/reduce_scatter | solution.py:100
  112.6 75.8 %reduce-scatter.9.cloned.1.call-done = f32[64,1024]{1,0:T(8,128)} async-done(((f32[512,1024]{1,0:T(8,128)}), f32[64,1024]{1,0:T(8,128)}) %reduce-scatter.9.cloned.1.call-update) | async-done | bytes 262160 | tf_op jit(solution)/shard_map/reduce_scatter | solution.py:130
  192.5 44.4 %all-gather.5.cloned.1.call-done = bf16[512,1024]{1,0:T(8,128)(2,1)} async-done(((bf16[64,1024]{1,0:T(8,128)(2,1)}), bf16[512,1024]{1,0:T(8,128)(2,1)}) %all-gather.5.cloned.1.call-update) | async-done | bytes 1048592 | tf_op jit(solution)/shard_map/all_gather | solution.py:137
  239.2 272.8 %while.39 = (s32[]{:T(128)}, f32[64,1024]{1,0:T(8,128)S(1)}, f32[27,64,512]{2,1,0:T(8,128)}, bf16[27,64,512]{2,1,0:T(8,128)(2,1)S(1)}, bf16[512,1024]{1,0:T(8,12...) while((s32[]{:T(128)}, f32[64,1024]{1,0:T(8,128)S(1)}, ...), condition=%wide.region_9.10_spmd.clone, body=%wide.region_8.9_spmd.clone.sunk | while | flops 456046592 | bytes 31054024 | solution.py:156
  265.7 5.8 dynamic_update_slice.27
  298.1 9.6 %dynamic_update_slice.27 = f32[27,64,512]{2,1,0:T(8,128)} dynamic-update-slice(f32[27,64,512]{2,1,0:T(8,128)} %get-tuple-element.591, f32[27,64,64]{2,1,0:T(8,128)S(1)} %convolution_bitcast_fusion.6, s32[]{:T(128)} %constant.1758.clone.1..sunk.1, s32[]{:T(128)} %constant.1758.clone.1..sunk.1, s32[]{:T(128)S(6)} %select_n.6693) | dynamic-update-slice | bytes 884740 | tf_op jit(solution)/shard_map/while/body/eval_jaxpr/dynamic_update_slice | solution.py:153
  334.3 5.8 dynamic_update_slice.27
  366.7 9.6 %dynamic_update_slice.27 = f32[27,64,512]{2,1,0:T(8,128)} dynamic-update-slice(f32[27,64,512]{2,1,0:T(8,128)} %get-tuple-element.591, f32[27,64,64]{2,1,0:T(8,128)S(1)} %convolution_bitcast_fusion.6, s32[]{:T(128)} %constant.1758.clone.1..sunk.1, s32[]{:T(128)} %constant.1758.clone.1..sunk.1, s32[]{:T(128)S(6)} %select_n.6693) | dynamic-update-slice | bytes 884740 | tf_op jit(solution)/shard_map/while/body/eval_jaxpr/dynamic_update_slice | solution.py:153
  402.8 5.8 dynamic_update_slice.27
  435.2 9.6 %dynamic_update_slice.27 = f32[27,64,512]{2,1,0:T(8,128)} dynamic-update-slice(f32[27,64,512]{2,1,0:T(8,128)} %get-tuple-element.591, f32[27,64,64]{2,1,0:T(8,128)S(1)} %convolution_bitcast_fusion.6, s32[]{:T(128)} %constant.1758.clone.1..sunk.1, s32[]{:T(128)} %constant.1758.clone.1..sunk.1, s32[]{:T(128)S(6)} %select_n.6693) | dynamic-update-slice | bytes 884740 | tf_op jit(solution)/shard_map/while/body/eval_jaxpr/dynamic_update_slice | solution.py:153
  471.4 5.2 dynamic_update_slice.27
  503.2 8.8 %dynamic_update_slice.27 = f32[27,64,512]{2,1,0:T(8,128)} dynamic-update-slice(f32[27,64,512]{2,1,0:T(8,128)} %get-tuple-element.591, f32[27,64,64]{2,1,0:T(8,128)S(1)} %convolution_bitcast_fusion.6, s32[]{:T(128)} %constant.1758.clone.1..sunk.1, s32[]{:T(128)} %constant.1758.clone.1..sunk.1, s32[]{:T(128)S(6)} %select_n.6693) | dynamic-update-slice | bytes 884740 | tf_op jit(solution)/shard_map/while/body/eval_jaxpr/dynamic_update_slice | solution.py:153
  514.3 139.8 %while.38 = (s32[]{:T(128)}, f32[64,1024]{1,0:T(8,128)}, f32[27,512,64]{1,2,0:T(8,128)}, bf16[27,512,64]{1,2,0:T(8,128)(2,1)}, bf16[512,1024]{1,0:T(8,128)(2,1)}...) while((s32[]{:T(128)}, f32[64,1024]{1,0:T(8,128)}, ...), condition=%wide.region_4.5_spmd.clone, body=%wide.region_3.4_spmd.clone.sunk | while | flops 456046592 | bytes 17422536 | solution.py:126
  521.9 6.1 dynamic_update_slice.26
  538.3 8.5 %dynamic_update_slice.26 = f32[27,512,64]{1,2,0:T(8,128)} dynamic-update-slice(f32[27,512,64]{1,2,0:T(8,128)} %get-tuple-element.561, f32[27,64,64]{1,2,0:T(8,128)} %fusion.406, s32[]{:T(128)} %constant.1758.clone.1..sunk, s32[]{:T(128)S(6)} %select_n.6557, s32[]{:T(128)} %constant.1758.clone.1..sunk) | dynamic-update-slice | bytes 884740 | tf_op jit(solution)/shard_map/while/body/eval_jaxpr/dynamic_update_slice | solution.py:123
  557.2 6.1 dynamic_update_slice.26
  573.6 8.5 %dynamic_update_slice.26 = f32[27,512,64]{1,2,0:T(8,128)} dynamic-update-slice(f32[27,512,64]{1,2,0:T(8,128)} %get-tuple-element.561, f32[27,64,64]{1,2,0:T(8,128)} %fusion.406, s32[]{:T(128)} %constant.1758.clone.1..sunk, s32[]{:T(128)S(6)} %select_n.6557, s32[]{:T(128)} %constant.1758.clone.1..sunk) | dynamic-update-slice | bytes 884740 | tf_op jit(solution)/shard_map/while/body/eval_jaxpr/dynamic_update_slice | solution.py:123
  592.5 6.1 dynamic_update_slice.26
  608.9 8.5 %dynamic_update_slice.26 = f32[27,512,64]{1,2,0:T(8,128)} dynamic-update-slice(f32[27,512,64]{1,2,0:T(8,128)} %get-tuple-element.561, f32[27,64,64]{1,2,0:T(8,128)} %fusion.406, s32[]{:T(128)} %constant.1758.clone.1..sunk, s32[]{:T(128)S(6)} %select_n.6557, s32[]{:T(128)} %constant.1758.clone.1..sunk) | dynamic-update-slice | bytes 884740 | tf_op jit(solution)/shard_map/while/body/eval_jaxpr/dynamic_update_slice | solution.py:123
  627.8 5.4 dynamic_update_slice.26
  643.6 7.7 dynamic_update_slice.26
  654.1 28.4 %psum.22 = f32[64]{0:T(128)S(1)} all-reduce(f32[64]{0:T(128)S(1)} %get-tuple-element.439), channel_id=1, replica_groups=mesh['dp'=16,'chan'=8] {'dp'}, use_global_device_ids=true, to_apply=%region_12.13 | all-reduce | flops 64 | bytes 512 | tf_op jit(solution)/shard_map/psum | solution.py:157
  684.4 107.9 %all-reduce.7.cloned.1.call-done = (f32[27,64,512]{2,1,0:T(8,128)}, f32[27,512,64]{1,2,0:T(8,128)}) async-done(((f32[27,64,512]{2,1,0:T(8,128)}, f32[27,512,64]{1,2,0:T(8,128)}), (f32[27,64,512]{2,1,0:T(8,128)}, f32[27,512,64]{1,2,0:T(8,128)})) %all-reduce.7.cloned.1.call-update) | async-done | bytes 7077904 | tf_op jit(solution)/shard_map/psum | solution.py:157
  (1073 shorter events, 340.4 us)
Async XLA Ops:
  7.2 13.5 %copy-start = (bf16[1,64,1024]{2,1,0:T(8,128)(2,1)S(1)}, bf16[1,64,1024]{2,1,0:T(8,128)(2,1)}, u32[]{:S(2)}) copy-start(bf16[1,64,1024]{2,1,0:T(8,128)(2,1)} %param.13) | copy-start | bytes 393220
  7.2 14.7 %copy-start.2 = (bf16[1,64,1024]{2,1,0:T(8,128)(2,1)S(1)}, bf16[1,64,1024]{2,1,0:T(8,128)(2,1)}, u32[]{:S(2)}) copy-start(bf16[1,64,1024]{2,1,0:T(8,128)(2,1)} %param.9) | copy-start | bytes 393220
  7.2 103.1 %reduce-scatter.7.cloned.1.call-start = ((), (), s32[]{:S(2)}) async-start(), calls=%async_computation.4 | async-start | bytes 2359296 | tf_op jit(solution)/shard_map/reduce_scatter | solution.py:100
  22.1 4.4 copy-start.9
  32.8 155.6 %reduce-scatter.9.cloned.1.call-start = ((), (), s32[]{:S(2)}) async-start(), calls=%async_computation.5 | async-start | bytes 2359296 | tf_op jit(solution)/shard_map/reduce_scatter | solution.py:130
  41.7 195.2 %all-gather.5.cloned.1.call-start = ((), (), s32[]{:S(2)}) async-start(), calls=%async_computation.3 | async-start | bytes 1179648 | tf_op jit(solution)/shard_map/all_gather | solution.py:137
  191.7 320.3 %all-gather.3.cloned.1.call-start = ((), (), s32[]{:S(2)}) async-start(), calls=%async_computation.2 | async-start | bytes 1179648 | tf_op jit(solution)/shard_map/all_gather | solution.py:107
  192.3 600.0 %all-reduce.7.cloned.1.call-start = ((), (), s32[]{:S(2)}) async-start(), calls=%async_computation.6 | async-start | bytes 14155776 | tf_op jit(solution)/shard_map/psum | solution.py:157
  330.1 3.1 copy-start.4
  362.5 3.1 copy-start.4
  398.6 3.1 copy-start.4
  431.0 3.1 copy-start.4
  467.2 3.1 copy-start.4
  515.2 4.0 copy-start.1
  531.6 4.0 copy-start.1
  550.5 4.0 copy-start.1
  566.9 4.0 copy-start.1
  585.8 4.0 copy-start.1
  602.2 4.0 copy-start.1
  621.1 4.0 copy-start.1
  636.9 4.0 copy-start.1
  654.0 29.0 %copy-start.7 = (f32[64,1024]{1,0:T(8,128)S(1)}, f32[64,1024]{1,0:T(8,128)}, u32[]{:S(2)}) copy-start(f32[64,1024]{1,0:T(8,128)} %copy-done.6) | copy-start | bytes 786436
  654.0 29.7 %copy-start.5 = (f32[64,1024]{1,0:T(8,128)S(1)}, f32[64,1024]{1,0:T(8,128)}, u32[]{:S(2)}) copy-start(f32[64,1024]{1,0:T(8,128)} %get-tuple-element.381) | copy-start | bytes 786436
  792.3 4.6 copy-start.8
  (6 other events, 15.9 us)
Sparse Core Ops, SparseCore 0:
  32.9 77.3 reduce-scatter.6
  114.6 73.7 reduce-scatter.8
  191.8 45.0 all-gather.4
  239.7 45.0 all-gather.2
  654.2 138.0 all-reduce.6
where the time goes:
time: 809 us; the launch traced here: 806 us
  waiting for transfers between devices  297 us (37%)
  other arithmetic  232 us (29%)
  local copies, waits for them, and re-layouts  145 us (18%)
  matrix products  86.1 us (11%)
  blocking collectives  28.4 us (4%)
  between operations  14.4 us (2%)
    while x416, other arithmetic  189 us
    psum x1, waiting for transfers between devices, shards(): lax.psum((first_grad, second_grad, gain_part), 'dp')  108 us
    reduce_scatter x1, waiting for transfers between devices, shards(): lax.psum_scatter(lax.dot_general(weights, target_cols, contract_second, p...  75.8 us
    reduce_scatter x1, waiting for transfers between devices, shards(): lax.psum_scatter(lax.dot_general(weights, volume_cols, contract_first, pr...  67.8 us
    dynamic_update_slice x8, local copies, waits for them, and re-layouts, first_one_block(): grad_now = lax.dynamic_update_slice_in_dim(grad_now, grad_part, begin, 2)  60.5 us
    dynamic_update_slice x8, local copies, waits for them, and re-layouts, second_one_block(): grad_now = lax.dynamic_update_slice_in_dim(grad_now, grad_part, begin, 1)  56.9 us
    all_gather x1, waiting for transfers between devices, shards(): grad_rows = lax.all_gather(dpre_own, 'chan', axis=0, tiled=True)  44.4 us
    psum x1, blocking collectives, shards(): lax.psum((first_grad, second_grad, gain_part), 'dp')  28.4 us
  transfers between devices with their start and end apart: 5, of which 4 were waited for; matrix products, arithmetic and copies ran while one was open for 36% of the time, Pallas kernels for 0%

commit v1 on v0

--- a/solution.py
+++ b/solution.py
@@ -134,7 +134,12 @@
         tiled=True,
     )
     gain_part, dpre_own = normalize_back(dact_own, normed, inverse, scaled, own_gain)
-    grad_rows = lax.all_gather(dpre_own, "chan", axis=0, tiled=True)
+    lanes = []
+    for _ in range(lax.axis_size("chan")):
+        lanes.append(dpre_own)
+    back = jnp.stack(lanes, 0)
+    g_now = lax.all_to_all(back, "chan", split_axis=0, concat_axis=0)
+    grad_rows = jnp.concatenate(g_now, 0)
     count = grad_rows.shape[0]
     first_step_rows = block_rows(count)
 

time: 809 us -> 770 us (0.952)
  waiting for transfers between devices: 297 us -> 267 us
    all_gather x1 -> x0, waiting for transfers between devices: 44.4 us -> none  [shards(): grad_rows = lax.all_gather(dpre_own, 'chan', axis=0, tiled=True)]
    all_to_all x0 -> x1, waiting for transfers between devices: none -> 14.9 us  [shards(): g_now = lax.all_to_all(back, 'chan', split_axis=0, concat_axis=0)]
where the time goes in v1:
time: 770 us; the launch traced here: 766 us
  waiting for transfers between devices  267 us (35%)
  other arithmetic  225 us (29%)
  local copies, waits for them, and re-layouts  139 us (18%)
  matrix products  86.6 us (11%)
  blocking collectives  27.5 us (4%)
  between operations  14.4 us (2%)
    while x416, other arithmetic  182 us
    psum x1, waiting for transfers between devices, shards(): lax.psum((first_grad, second_grad, gain_part), 'dp')  107 us
    reduce_scatter x1, waiting for transfers between devices, shards(): lax.psum_scatter(lax.dot_general(weights, target_cols, contract_second, p...  75.8 us
    reduce_scatter x1, waiting for transfers between devices, shards(): lax.psum_scatter(lax.dot_general(weights, volume_cols, contract_first, pr...  68.4 us
    dynamic_update_slice x8, local copies, waits for them, and re-layouts, first_one_block(): grad_now = lax.dynamic_update_slice_in_dim(grad_now, grad_part, begin, 2)  60.5 us
    dynamic_update_slice x8, local copies, waits for them, and re-layouts, second_one_block(): grad_now = lax.dynamic_update_slice_in_dim(grad_now, grad_part, begin, 1)  56.9 us
    psum x1, blocking collectives, shards(): lax.psum((first_grad, second_grad, gain_part), 'dp')  27.5 us
    dot_general x8, matrix products, first_one_block(): lax.dot_general(weights, cols, contract_second, preferred_element_type=jn...  25.9 us
  transfers between devices with their start and end apart: 5, of which 4 were waited for; matrix products, arithmetic and copies ran while one was open for 36% of the time, Pallas kernels for 0%

profile of v1, /device:TPU:0, one launch (start us, length us, event | category | flops | bytes accessed | tf_op | source)
XLA Modules:
  0.0 766.4 jit_solution(3592475542503963388)
XLA Ops:
  33.0 5.4 convolution_bitcast_fusion.3
  42.1 68.4 %reduce-scatter.7.cloned.1.call-done = f32[64,1024]{1,0:T(8,128)} async-done(((f32[512,1024]{1,0:T(8,128)}), f32[64,1024]{1,0:T(8,128)}) %reduce-scatter.7.cloned.1.call-update) | async-done | bytes 262160 | tf_op jit(solution)/shard_map/reduce_scatter | solution.py:100
  112.7 75.8 %reduce-scatter.9.cloned.1.call-done = f32[64,1024]{1,0:T(8,128)} async-done(((f32[512,1024]{1,0:T(8,128)}), f32[64,1024]{1,0:T(8,128)}) %reduce-scatter.9.cloned.1.call-update) | async-done | bytes 262160 | tf_op jit(solution)/shard_map/reduce_scatter | solution.py:130
  197.8 14.9 %all-to-all-done = bf16[8,64,1024]{2,1,0:T(8,128)(2,1)S(1)} async-done(((bf16[8,64,1024]{2,1,0:T(8,128)(2,1)}), bf16[8,64,1024]{2,1,0:T(8,128)(2,1)S(1)}, u32[]{:S(2)}, u32[]{:S(2)}) %all-to-all-start) | async-done | bytes 1048608 | tf_op jit(solution)/shard_map/all_to_all | solution.py:141
  215.0 259.6 %while.39 = (s32[]{:T(128)}, f32[64,1024]{1,0:T(8,128)S(1)}, f32[27,64,512]{2,1,0:T(8,128)}, bf16[27,64,512]{2,1,0:T(8,128)(2,1)}, bf16[512,1024]{1,0:T(8,128)(2...) while((s32[]{:T(128)}, f32[64,1024]{1,0:T(8,128)S(1)}, ...), condition=%wide.region_9.10_spmd.clone, body=%wide.region_8.9_spmd.clone.sunk | while | flops 456046592 | bytes 31054024 | solution.py:161
  239.8 5.8 dynamic_update_slice.27
  270.6 9.6 %dynamic_update_slice.27 = f32[27,64,512]{2,1,0:T(8,128)} dynamic-update-slice(f32[27,64,512]{2,1,0:T(8,128)} %get-tuple-element.585, f32[27,64,64]{2,1,0:T(8,128)S(1)} %convolution_bitcast_fusion.6, s32[]{:T(128)} %constant.1758.clone.1..sunk.1, s32[]{:T(128)} %constant.1758.clone.1..sunk.1, s32[]{:T(128)S(6)} %select_n.6693) | dynamic-update-slice | bytes 884740 | tf_op jit(solution)/shard_map/while/body/eval_jaxpr/dynamic_update_slice | solution.py:158
  305.1 5.8 dynamic_update_slice.27
  335.8 9.6 %dynamic_update_slice.27 = f32[27,64,512]{2,1,0:T(8,128)} dynamic-update-slice(f32[27,64,512]{2,1,0:T(8,128)} %get-tuple-element.585, f32[27,64,64]{2,1,0:T(8,128)S(1)} %convolution_bitcast_fusion.6, s32[]{:T(128)} %constant.1758.clone.1..sunk.1, s32[]{:T(128)} %constant.1758.clone.1..sunk.1, s32[]{:T(128)S(6)} %select_n.6693) | dynamic-update-slice | bytes 884740 | tf_op jit(solution)/shard_map/while/body/eval_jaxpr/dynamic_update_slice | solution.py:158
  370.3 5.8 dynamic_update_slice.27
  401.1 9.6 %dynamic_update_slice.27 = f32[27,64,512]{2,1,0:T(8,128)} dynamic-update-slice(f32[27,64,512]{2,1,0:T(8,128)} %get-tuple-element.585, f32[27,64,64]{2,1,0:T(8,128)S(1)} %convolution_bitcast_fusion.6, s32[]{:T(128)} %constant.1758.clone.1..sunk.1, s32[]{:T(128)} %constant.1758.clone.1..sunk.1, s32[]{:T(128)S(6)} %select_n.6693) | dynamic-update-slice | bytes 884740 | tf_op jit(solution)/shard_map/while/body/eval_jaxpr/dynamic_update_slice | solution.py:158
  435.6 5.2 dynamic_update_slice.27
  465.7 8.8 %dynamic_update_slice.27 = f32[27,64,512]{2,1,0:T(8,128)} dynamic-update-slice(f32[27,64,512]{2,1,0:T(8,128)} %get-tuple-element.585, f32[27,64,64]{2,1,0:T(8,128)S(1)} %convolution_bitcast_fusion.6, s32[]{:T(128)} %constant.1758.clone.1..sunk.1, s32[]{:T(128)} %constant.1758.clone.1..sunk.1, s32[]{:T(128)S(6)} %select_n.6693) | dynamic-update-slice | bytes 884740 | tf_op jit(solution)/shard_map/while/body/eval_jaxpr/dynamic_update_slice | solution.py:158
  476.8 139.6 %while.38 = (s32[]{:T(128)}, f32[64,1024]{1,0:T(8,128)}, f32[27,512,64]{1,2,0:T(8,128)}, bf16[27,512,64]{1,2,0:T(8,128)(2,1)}, bf16[512,1024]{1,0:T(8,128)(2,1)}...) while((s32[]{:T(128)}, f32[64,1024]{1,0:T(8,128)}, ...), condition=%wide.region_4.5_spmd.clone, body=%wide.region_3.4_spmd.clone.sunk | while | flops 456046592 | bytes 17422536 | solution.py:126
  484.4 6.1 dynamic_update_slice.26
  500.8 8.5 %dynamic_update_slice.26 = f32[27,512,64]{1,2,0:T(8,128)} dynamic-update-slice(f32[27,512,64]{1,2,0:T(8,128)} %get-tuple-element.555, f32[27,64,64]{1,2,0:T(8,128)} %fusion.406, s32[]{:T(128)} %constant.1758.clone.1..sunk, s32[]{:T(128)S(6)} %select_n.6557, s32[]{:T(128)} %constant.1758.clone.1..sunk) | dynamic-update-slice | bytes 884740 | tf_op jit(solution)/shard_map/while/body/eval_jaxpr/dynamic_update_slice | solution.py:123
  519.6 6.1 dynamic_update_slice.26
  536.1 8.5 %dynamic_update_slice.26 = f32[27,512,64]{1,2,0:T(8,128)} dynamic-update-slice(f32[27,512,64]{1,2,0:T(8,128)} %get-tuple-element.555, f32[27,64,64]{1,2,0:T(8,128)} %fusion.406, s32[]{:T(128)} %constant.1758.clone.1..sunk, s32[]{:T(128)S(6)} %select_n.6557, s32[]{:T(128)} %constant.1758.clone.1..sunk) | dynamic-update-slice | bytes 884740 | tf_op jit(solution)/shard_map/while/body/eval_jaxpr/dynamic_update_slice | solution.py:123
  554.9 6.1 dynamic_update_slice.26
  571.4 8.5 %dynamic_update_slice.26 = f32[27,512,64]{1,2,0:T(8,128)} dynamic-update-slice(f32[27,512,64]{1,2,0:T(8,128)} %get-tuple-element.555, f32[27,64,64]{1,2,0:T(8,128)} %fusion.406, s32[]{:T(128)} %constant.1758.clone.1..sunk, s32[]{:T(128)S(6)} %select_n.6557, s32[]{:T(128)} %constant.1758.clone.1..sunk) | dynamic-update-slice | bytes 884740 | tf_op jit(solution)/shard_map/while/body/eval_jaxpr/dynamic_update_slice | solution.py:123
  590.2 5.4 dynamic_update_slice.26
  606.0 7.7 %dynamic_update_slice.26 = f32[27,512,64]{1,2,0:T(8,128)} dynamic-update-slice(f32[27,512,64]{1,2,0:T(8,128)} %get-tuple-element.555, f32[27,64,64]{1,2,0:T(8,128)} %fusion.406, s32[]{:T(128)} %constant.1758.clone.1..sunk, s32[]{:T(128)S(6)} %select_n.6557, s32[]{:T(128)} %constant.1758.clone.1..sunk) | dynamic-update-slice | bytes 884740 | tf_op jit(solution)/shard_map/while/body/eval_jaxpr/dynamic_update_slice | solution.py:123
  616.4 27.5 %psum.22 = f32[64]{0:T(128)S(1)} all-reduce(f32[64]{0:T(128)S(1)} %get-tuple-element.433), channel_id=1, replica_groups=mesh['dp'=16,'chan'=8] {'dp'}, use_global_device_ids=true, to_apply=%region_12.13 | all-reduce | flops 64 | bytes 512 | tf_op jit(solution)/shard_map/psum | solution.py:162
  645.8 107.2 %all-reduce.7.cloned.1.call-done = (f32[27,64,512]{2,1,0:T(8,128)}, f32[27,512,64]{1,2,0:T(8,128)}) async-done(((f32[27,64,512]{2,1,0:T(8,128)}, f32[27,512,64]{1,2,0:T(8,128)}), (f32[27,64,512]{2,1,0:T(8,128)}, f32[27,512,64]{1,2,0:T(8,128)})) %all-reduce.7.cloned.1.call-update) | async-done | bytes 7077904 | tf_op jit(solution)/shard_map/psum | solution.py:162
  (1075 shorter events, 332.2 us)
Async XLA Ops:
  7.2 13.5 %copy-start = (bf16[1,64,1024]{2,1,0:T(8,128)(2,1)S(1)}, bf16[1,64,1024]{2,1,0:T(8,128)(2,1)}, u32[]{:S(2)}) copy-start(bf16[1,64,1024]{2,1,0:T(8,128)(2,1)} %param.13) | copy-start | bytes 393220
  7.2 14.7 %copy-start.2 = (bf16[1,64,1024]{2,1,0:T(8,128)(2,1)S(1)}, bf16[1,64,1024]{2,1,0:T(8,128)(2,1)}, u32[]{:S(2)}) copy-start(bf16[1,64,1024]{2,1,0:T(8,128)(2,1)} %param.9) | copy-start | bytes 393220
  7.2 103.3 %reduce-scatter.7.cloned.1.call-start = ((), (), s32[]{:S(2)}) async-start(), calls=%async_computation.4 | async-start | bytes 2359296 | tf_op jit(solution)/shard_map/reduce_scatter | solution.py:100
  22.1 4.4 copy-start.9
  32.9 155.6 %reduce-scatter.9.cloned.1.call-start = ((), (), s32[]{:S(2)}) async-start(), calls=%async_computation.5 | async-start | bytes 2359296 | tf_op jit(solution)/shard_map/reduce_scatter | solution.py:130
  192.9 19.8 %all-to-all-start = ((bf16[8,64,1024]{2,1,0:T(8,128)(2,1)}), bf16[8,64,1024]{2,1,0:T(8,128)(2,1)S(1)}, u32[]{:S(2)}, u32[]{:S(2)}) async-start(bf16[8,64,1024]{2,1,0:T(8,128)(2,1)} %stack.2), calls=%async_computation | async-start | bytes 2097152 | tf_op jit(solution)/shard_map/all_to_all | solution.py:141
  196.8 277.7 %all-gather.2.cloned.1.call-start = ((), (), s32[]{:S(2)}) async-start(), calls=%async_computation.3 | async-start | bytes 1179648 | tf_op jit(solution)/shard_map/all_gather | solution.py:107
  197.6 555.5 %all-reduce.7.cloned.1.call-start = ((), (), s32[]{:S(2)}) async-start(), calls=%async_computation.6 | async-start | bytes 14155776 | tf_op jit(solution)/shard_map/psum | solution.py:162
  235.5 3.3 copy-start.4
  266.2 3.3 copy-start.4
  300.8 3.3 copy-start.4
  366.0 3.3 copy-start.4
  431.2 3.3 copy-start.4
  477.7 4.0 copy-start.1
  494.1 4.0 copy-start.1
  512.9 4.0 copy-start.1
  529.4 4.0 copy-start.1
  548.2 4.0 copy-start.1
  564.7 4.0 copy-start.1
  583.5 4.0 copy-start.1
  599.3 4.0 copy-start.1
  616.4 28.1 %copy-start.7 = (f32[64,1024]{1,0:T(8,128)S(1)}, f32[64,1024]{1,0:T(8,128)}, u32[]{:S(2)}) copy-start(f32[64,1024]{1,0:T(8,128)} %copy-done.6) | copy-start | bytes 786436
  616.4 28.8 %copy-start.5 = (f32[64,1024]{1,0:T(8,128)S(1)}, f32[64,1024]{1,0:T(8,128)}, u32[]{:S(2)}) copy-start(f32[64,1024]{1,0:T(8,128)} %get-tuple-element.381) | copy-start | bytes 786436
  753.1 4.6 copy-start.8
  (7 other events, 19.5 us)
Sparse Core Ops, SparseCore 0:
  33.0 77.3 reduce-scatter.6
  114.7 73.7 reduce-scatter.8
  200.6 48.3 all-gather.1
  616.6 136.4 all-reduce.6
